TPU v7x, 32 devices: a whole 2x2x4 slice. The times are simulated.
32 devices in a mesh: blk: 8 (over z, x), aux: 4 (over y, core).
Axes of the slice: x: 2, y: 2, z: 4, core: 2. Of those that a mesh axis runs over, the one named last changes fastest.
Arguments:
- half_ints: bfloat16 [32, 1536, 384], P('blk', 'aux'), may hold values from -0.625 to 0.625
- metric_inv: bfloat16 [1536, 1536], P('aux'), may hold values from -1 to 2, as said below
- occ_energy: float32 [32], replicated, may hold values from -2 to -0.3
- vir_energy: float32 [384], replicated, may hold values from 0.3 to 3
Outputs:
- gamma: bfloat16 [32, 1536, 384], P('blk', 'aux')
Inputs may be any that keep to these rules, and one draw needn't show every extreme that they name: metric_inv is lower triangular (zero where Q > P) with a positive diagonal.
All inputs are finite; a program needn't handle non-finite values.
Results may differ from a plain program's by a relative error of at most 0.0058.
Values may be sent and summed in bfloat16 or wider, within the bound.
A program may use at most 64 MiB of HBM per device.

v0:
```python
import jax
import jax.numpy as jnp
from jax import lax
from jax.sharding import PartitionSpec as P

CYCLE = 4


def shifted(block, axis, distance):
    devices = range(lax.axis_size(axis))
    route = [((i - distance) % len(devices), i) for i in devices]
    return lax.ppermute(block, axis, route)


def local(half_ints, metric_inv, occ_energy, vir_energy):
    groups = lax.axis_size("aux")
    block_count = lax.axis_size("blk")
    per_block = half_ints.shape[0]
    per_group = per_block // groups
    naux_all = metric_inv.shape[1]
    vir_count = half_ints.shape[2]
    regrouped = lax.all_to_all(half_ints, "aux", split_axis=0, concat_axis=1, tiled=True)
    own_start = lax.axis_index("blk") * per_block + lax.axis_index("aux") * per_group
    own_energy = lax.dynamic_slice_in_dim(occ_energy, own_start, per_group)
    empty_fit = jnp.zeros((per_group, naux_all, vir_count), jnp.float32)
    fitted = jnp.einsum(
        "pq,upa->uqa",
        lax.all_gather(metric_inv, "aux", axis=0, tiled=True),
        regrouped,
        preferred_element_type=jnp.float32,
    ).astype(jnp.bfloat16)

    def contribute(density_acc, partner, cycle_step):
        partner_start = (
            lax.axis_index("blk") - cycle_step
        ) % block_count * per_block + lax.axis_index("aux") * per_group
        partner_energy = lax.dynamic_slice_in_dim(occ_energy, partner_start, per_group)
        pair_ints = jnp.einsum("uqa,vqb->uvab", fitted, partner, preferred_element_type=jnp.float32)
        energy_gap = (
            own_energy[:, None, None, None]
            + partner_energy[None, :, None, None]
            - vir_energy[None, None, :, None]
            - vir_energy[None, None, None, :]
        )
        amplitude = ((2.0 * pair_ints - jnp.swapaxes(pair_ints, 2, 3)) / energy_gap).astype(
            jnp.bfloat16
        )
        return density_acc + jnp.einsum(
            "uvab,vqb->uqa", amplitude, partner, preferred_element_type=jnp.float32
        )

    density_acc = contribute(empty_fit, fitted, 0)
    moving = fitted
    for cycle_step in range(1, CYCLE):
        moving = shifted(moving, "blk", 1)
        density_acc = contribute(density_acc, moving, cycle_step)
    density_fit = density_acc.astype(jnp.bfloat16)
    gamma_local = jnp.einsum(
        "pq,uqa->upa",
        lax.all_gather(metric_inv, "aux", axis=0, tiled=True),
        density_fit,
        preferred_element_type=jnp.float32,
    ).astype(jnp.bfloat16)
    return lax.all_to_all(gamma_local, "aux", split_axis=1, concat_axis=0, tiled=True)


def solution(mesh):
    placed = (P("blk", "aux", None), P("aux", None), P(), P())
    return jax.shard_map(
        local, mesh=mesh, in_specs=placed, out_specs=P("blk", "aux", None), check_vma=False
    )
```

profile of v0, /device:TPU:0, one launch (start us, length us, event | category | flops | bytes accessed | tf_op | source)
XLA Modules:
  0.0 199.4 jit_solution(6540370813569139194)
XLA Ops:
  6.5 0.7 all-gather.2.cloned.1.call-update
  7.3 0.5 copy-done.1
  7.8 25.9 %all_to_all.21 = bf16[4,384,384]{2,1,0:T(8,128)(2,1)S(1)} all-to-all(bf16[4,384,384]{2,1,0:T(8,128)(2,1)S(1)} %copy-done.1), channel_id=1, replica_groups=mesh['blk'=8,'aux'=4] {'aux'}, dimensions={0} | all-to-all | bytes 2359296 | tf_op jit(solution)/shard_map/all_to_all | solution.py:22
  33.7 20.9 %all-gather.2.cloned.1.call-done = bf16[1536,1536]{1,0:T(8,128)(2,1)} async-done(((bf16[384,1536]{1,0:T(8,128)(2,1)}), bf16[1536,1536]{1,0:T(8,128)(2,1)}) %all-gather.2.cloned.1.call-update) | async-done | bytes 4718608 | tf_op jit(solution)/shard_map/all_gather | solution.py:28
  54.6 4.4 %convolution_convert_fusion.1 = bf16[384,1536]{1,0:T(8,128)(2,1)S(1)} fusion(bf16[1536,384]{1,0:T(8,128)(2,1)S(1)} %bitcast.132, bf16[1536,1536]{1,0:T(8,128)(2,1)} %all-gather.2.cloned.1.call-done), kind=kOutput, calls=%fused_computation.5 | convolution fusion | flops 1812529152 | bytes 7077888 | tf_op jit(solution)/shard_map/pq,upa->uqa/dot_general | solution.py:26
  59.0 1.5 collective-permute-start
  60.6 29.4 %collective-permute-done = bf16[1,1536,384]{1,2,0:T(8,128)(2,1)S(1)} collective-permute-done((bf16[1,1536,384]{1,2,0:T(8,128)(2,1)S(1)}, bf16[1,1536,384]{1,2,0:T(8,128)(2,1)S(1)}, u32[]{:S(2)}, u32[]{:S(2)}) %collective-permute-start) | collective-permute-done | bytes 1179680 | tf_op jit(solution)/shard_map/ppermute | solution.py:12
  90.0 0.8 fusion.51
  96.3 0.8 fusion.16
  97.3 2.4 %fusion.14 = f32[1536,384]{1,0:T(8,128)} fusion(bf16[384,1536]{1,0:T(8,128)(2,1)S(1)} %convolution_convert_fusion.1, f32[384,384]{1,0:T(8,128)S(1)} %fusion.16, f32[384,384]{0,1:T(8,128)S(1)} %copy.21, f32[384]{0:T(512)S(1)} %copy-done.7, f32[384]{0:T(512)S(1)} %get-tuple-element.7), kind=kOutput, calls=%fused_computation.19 | convolution fusion | flops 453722112 | bytes 4721664 | tf_op jit(solution)/shard_map/uvab,vqb->uqa/dot_general | solution.py:48
  99.8 20.4 %collective-permute-done.1 = bf16[1,1536,384]{1,2,0:T(8,128)(2,1)} collective-permute-done((bf16[1,1536,384]{1,2,0:T(8,128)(2,1)S(1)}, bf16[1,1536,384]{1,2,0:T(8,128)(2,1)}, u32[]{:S(2)}, u32[]{:S(2)}) %collective-permute-start.1) | collective-permute-done | bytes 1179680 | tf_op jit(solution)/shard_map/ppermute | solution.py:12
  120.1 2.1 %fusion.9 = f32[384,384]{1,0:T(8,128)S(1)} fusion(bf16[1,1536,384]{1,2,0:T(8,128)(2,1)S(1)} %collective-permute-done, bf16[384,1536]{1,0:T(8,128)(2,1)} %copy-done.2), kind=kOutput, calls=%fused_computation.14 | convolution fusion | flops 452984832 | bytes 2949120 | tf_op jit(solution)/shard_map/uqa,vqb->uvab/dot_general | solution.py:38
  122.4 3.1 %convolution_add_fusion.2 = f32[1536,384]{1,0:T(8,128)S(1)} fusion(f32[1536,384]{1,0:T(8,128)} %fusion.14, bf16[1,1536,384]{1,2,0:T(8,128)(2,1)} %copy-done.5, f32[384,384]{1,0:T(8,128)S(1)} %fusion.9, f32[384,384]{0,1:T(8,128)S(1)} %copy.23, f32[384]{0:T(512)S(1)} %copy-done.7, f32[384]{0:T(512)S(1)} %get-tuple-element.6), kind=kOutput, calls=%fused_computation.2 | convolution fusion | flops 454311936 | bytes 7080960 | tf_op jit(solution)/shard_map/uvab,vqb->uqa/dot_general | solution.py:48
  125.6 2.1 %fusion.6 = f32[384,384]{1,0:T(8,128)S(1)} fusion(bf16[1,1536,384]{1,2,0:T(8,128)(2,1)} %collective-permute-done.1, bf16[384,1536]{1,0:T(8,128)(2,1)S(1)} %copy-done.3), kind=kOutput, calls=%fused_computation.11 | convolution fusion | flops 452984832 | bytes 2949120 | tf_op jit(solution)/shard_map/uqa,vqb->uvab/dot_general | solution.py:38
  127.9 3.8 %convolution_add_fusion.1 = f32[1536,384]{1,0:T(8,128)} fusion(f32[1536,384]{1,0:T(8,128)S(1)} %convolution_add_fusion.2, bf16[1,1536,384]{1,2,0:T(8,128)(2,1)} %collective-permute-done.1, f32[384,384]{1,0:T(8,128)S(1)} %fusion.6, f32[384,384]{0,1:T(8,128)S(1)} %copy.25, f32[384]{0:T(512)S(1)} %copy-done.7, f32[384]{0:T(512)S(1)} %get-tuple-element.8), kind=kOutput, calls=%fused_computation.1 | convolution fusion | flops 454311936 | bytes 7080960 | tf_op jit(solution)/shard_map/uvab,vqb->uqa/dot_general | solution.py:48
  131.7 18.0 %collective-permute-done.2 = bf16[1,1536,384]{1,2,0:T(8,128)(2,1)} collective-permute-done((bf16[1,1536,384]{1,2,0:T(8,128)(2,1)}, bf16[1,1536,384]{1,2,0:T(8,128)(2,1)}, u32[]{:S(2)}, u32[]{:S(2)}) %collective-permute-start.2) | collective-permute-done | bytes 1179680 | tf_op jit(solution)/shard_map/ppermute | solution.py:12
  149.6 2.2 %fusion.3 = f32[384,384]{1,0:T(8,128)S(1)} fusion(bf16[1,1536,384]{1,2,0:T(8,128)(2,1)} %collective-permute-done.2, bf16[384,1536]{1,0:T(8,128)(2,1)S(1)} %copy-done.4), kind=kOutput, calls=%fused_computation.8 | convolution fusion | flops 452984832 | bytes 2949120 | tf_op jit(solution)/shard_map/uqa,vqb->uvab/dot_general | solution.py:38
  151.9 1.0 copy.27
  152.9 5.9 %fusion.1 = bf16[1,1536,384]{1,2,0:T(8,128)(2,1)S(1)} fusion(bf16[1536,1536]{1,0:T(8,128)(2,1)} %all-gather.2.cloned.1.call-done, f32[1536,384]{1,0:T(8,128)S(1)} %copy-done, bf16[1,1536,384]{1,2,0:T(8,128)(2,1)} %collective-permute-done.2, f32[384,384]{1,0:T(8,128)} %copy-done.6, f32[384,384]{0,1:T(8,128)} %copy.27, f32[384]{0:T(512)S(1)} %copy-done.9, ...), kind=kOutput, calls=%fused_computation.6 | convolution fusion | flops 2267430912 | bytes 10619904 | tf_op jit(solution)/shard_map/pq,uqa->upa/dot_general | solution.py:58
  158.8 3.3 %copy.28 = bf16[1,1536,384]{2,0,1:T(2,128)(2,1)S(1)} copy(bf16[1,1536,384]{1,2,0:T(8,128)(2,1)S(1)} %fusion.1) | data formatting | bytes 2359296 | tf_op jit(solution)/shard_map/convert_element_type | solution.py:63
  162.6 9.1 %reduce = bf16[1536,384]{1,0:T(8,128)(2,1)S(1)} reduce(bf16[1536,1,384]{2,1,0:T(2,128)(2,1)S(1)} %bitcast.130, bf16[]{:T(256)} %broadcast.220), dimensions={1}, to_apply=%bitcast.125.reduce_sub_computation | reduce | bytes 2359298
  172.0 18.3 %all_to_all.22 = bf16[4,2,73728]{2,1,0:T(2,128)(2,1)S(1)} all-to-all(bf16[4,2,73728]{2,1,0:T(2,128)(2,1)S(1)} %reshape.285), channel_id=1, replica_groups=mesh['blk'=8,'aux'=4] {'aux'}, dimensions={0} | all-to-all | bytes 2359296 | tf_op jit(solution)/shard_map/all_to_all | solution.py:64
  190.3 1.1 reshape.286
  191.4 1.2 copy.29
  (28 shorter events, 2.2 us)
Async XLA Ops:
  6.5 1.3 copy-start.1
  6.5 48.1 %all-gather.2.cloned.1.call-start = ((), (), s32[]{:S(2)}) async-start(), calls=%async_computation.2 | async-start | bytes 5898240 | tf_op jit(solution)/shard_map/all_gather | solution.py:28
  54.6 35.4 %copy-start.8 = (f32[32]{0:T(128)S(1)}, f32[32]{0:T(128)}, u32[]{:S(2)}) copy-start(f32[32]{0:T(128)} %param.6) | copy-start | bytes 388
  54.6 41.1 %copy-start.7 = (f32[384]{0:T(512)S(1)}, f32[384]{0:T(512)}, u32[]{:S(2)}) copy-start(f32[384]{0:T(512)} %param.7) | copy-start | bytes 4612
  59.0 38.3 %copy-start.2 = (bf16[384,1536]{1,0:T(8,128)(2,1)}, bf16[384,1536]{1,0:T(8,128)(2,1)S(1)}, u32[]{:S(2)}) copy-start(bf16[384,1536]{1,0:T(8,128)(2,1)S(1)} %convolution_convert_fusion.1) | copy-start | bytes 3538948
  59.0 31.0 %collective-permute-start = (bf16[1,1536,384]{1,2,0:T(8,128)(2,1)S(1)}, bf16[1,1536,384]{1,2,0:T(8,128)(2,1)S(1)}, u32[]{:S(2)}, u32[]{:S(2)}) collective-permute-start(bf16[1,1536,384]{1,2,0:T(8,128)(2,1)S(1)} %bitcast.133), channel_id=1, source_target_pairs={{28,0},{0,4},{4,8},{8,12},{12,16},{16,20},{20,24},{24,28},{29,1},{... | collective-permute-start | bytes 3538952 | tf_op jit(solution)/shard_map/ppermute | solution.py:12
  90.0 30.2 %copy-start.5 = (bf16[1,1536,384]{1,2,0:T(8,128)(2,1)}, bf16[1,1536,384]{1,2,0:T(8,128)(2,1)S(1)}, u32[]{:S(2)}) copy-start(bf16[1,1536,384]{1,2,0:T(8,128)(2,1)S(1)} %collective-permute-done) | copy-start | bytes 3538948
  90.0 30.1 %collective-permute-start.1 = (bf16[1,1536,384]{1,2,0:T(8,128)(2,1)S(1)}, bf16[1,1536,384]{1,2,0:T(8,128)(2,1)}, u32[]{:S(2)}, u32[]{:S(2)}) collective-permute-start(bf16[1,1536,384]{1,2,0:T(8,128)(2,1)S(1)} %collective-permute-done), channel_id=1, source_target_pairs={{28,0},{0,4},{4,8},{8,12},{12,16},{16,20},{20,24},{24,28},{29,1},{... | collective-permute-start | bytes 3538952 | tf_op jit(solution)/shard_map/ppermute | solution.py:12
  120.1 29.5 %collective-permute-start.2 = (bf16[1,1536,384]{1,2,0:T(8,128)(2,1)}, bf16[1,1536,384]{1,2,0:T(8,128)(2,1)}, u32[]{:S(2)}, u32[]{:S(2)}) collective-permute-start(bf16[1,1536,384]{1,2,0:T(8,128)(2,1)} %collective-permute-done.1), channel_id=1, source_target_pairs={{28,0},{0,4},{4,8},{8,12},{12,16},{16,20},{20,24},{24,28},{29,1},{... | collective-permute-start | bytes 3538952 | tf_op jit(solution)/shard_map/ppermute | solution.py:12
  122.4 3.1 %copy-start.3 = (bf16[384,1536]{1,0:T(8,128)(2,1)S(1)}, bf16[384,1536]{1,0:T(8,128)(2,1)}, u32[]{:S(2)}) copy-start(bf16[384,1536]{1,0:T(8,128)(2,1)} %copy-done.2) | copy-start | bytes 3538948
  127.9 21.8 %copy-start.4 = (bf16[384,1536]{1,0:T(8,128)(2,1)S(1)}, bf16[384,1536]{1,0:T(8,128)(2,1)}, u32[]{:S(2)}) copy-start(bf16[384,1536]{1,0:T(8,128)(2,1)} %copy-done.2) | copy-start | bytes 3538948
  149.6 3.3 %copy-start = (f32[1536,384]{1,0:T(8,128)S(1)}, f32[1536,384]{1,0:T(8,128)}, u32[]{:S(2)}) copy-start(f32[1536,384]{1,0:T(8,128)} %convolution_add_fusion.1) | copy-start | bytes 7077892
  151.8 1.1 copy-start.6
  151.8 1.1 copy-start.9
Sparse Core Ops, SparseCore 0:
  8.9 45.6 all-gather.1
where the time goes:
time: 200 us; the launch traced here: 199 us
  waiting for transfers between devices  89.3 us (45%)
  blocking collectives  44.2 us (22%)
  matrix products  26.7 us (13%)
  between operations  18.5 us (9%)
  other arithmetic  9.59 us (5%)
  local copies, waits for them, and re-layouts  9.57 us (5%)
    ppermute x3, waiting for transfers between devices, shifted(): return lax.ppermute(block, axis, route)  67.7 us
    all_to_all x1, blocking collectives, local(): lax.all_to_all(half_ints, 'aux', split_axis=0, concat_axis=1, tiled=True)  25.9 us
    all_gather x1, waiting for transfers between devices, local(): lax.all_gather(metric_inv, 'aux', axis=0, tiled=True)  20.9 us
    all_to_all x1, blocking collectives, local(): lax.all_to_all(gamma_local, 'aux', split_axis=1, concat_axis=0, tiled=True)  18.3 us
    dot_general x3, matrix products, contribute(): jnp.einsum('uvab,vqb->uqa', amplitude, partner, preferred_element_type=jn...  9.35 us
    unnamed x1, other arithmetic  9.05 us
    dot_general x4, matrix products, contribute(): jnp.einsum('uqa,vqb->uvab', fitted, partner, preferred_element_type=jnp.f...  7.11 us
    dot_general x1, matrix products, local(): jnp.einsum('pq,uqa->upa', lax.all_gather(metric_inv, 'aux', axis=0, tiled...  5.9 us
  transfers between devices with their start and end apart: 4, of which 4 were waited for; matrix products, arithmetic and copies ran while one was open for 8% of the time, Pallas kernels for 0%

commit v1 on v0

v1 whole, which is shorter than its diff:
```python
import functools

import jax
import jax.numpy as jnp
from jax import lax
from jax.experimental import pallas as pl
from jax.experimental.pallas import tpu as pltpu
from jax.sharding import PartitionSpec as P

CYCLE = 4
MESH = pl.DeviceIdType.MESH


def kernel(
    blocks, groups, tile,
    ints_ref, metric_ref, occ_ref, vir_ref,
    out_ref,
    ints, metric, metric_t, fit, fit_t, gap, dens, dens_b, gam,
    h_send, h_recv, z_send, c_send, f_send, w_send, ring_recv,
    m1_send, m1_recv, m2_send, m2_recv, m3_send, m3_recv, own_sem, g_send, g_recv,
):
    shard = ints_ref.shape[1]
    half = shard // 2
    naux = metric_ref.shape[1]
    vir = ints_ref.shape[2]
    tiles = naux // tile
    pairs = groups // 2
    b, g = lax.axis_index("blk"), lax.axis_index("aux")
    x, core, h = b % 2, g % 2, g // 2
    plane, mate, ahead = b - x, g + 1 - 2 * core, (b + 2) % blocks
    across = b + 1 - 2 * x
    own_b, own_c = plane + core, g - core + x

    def rows(p):
        return pl.ds(pl.multiple_of(p * shard, shard), shard)

    def halves(p, which):
        return pl.ds(pl.multiple_of(p * shard + which * half, half), half)

    def width(hv):
        return min(naux, -(-2 * shard * (hv + 1) // tile) * tile)

    def remote(src, dst, send, recv, device):
        return pltpu.make_async_remote_copy(
            src_ref=src, dst_ref=dst, send_sem=send, recv_sem=recv,
            device_id=device, device_id_type=MESH,
        )

    def landed(dst, recv):
        pltpu.make_async_copy(dst, dst, recv).wait()

    barrier = pltpu.get_barrier_semaphore()
    for xx in range(2):
        for gg in range(groups):
            @pl.when((plane + xx != b) | (gg != g))
            def _():
                pl.semaphore_signal(barrier, inc=1, device_id=(plane + xx, gg), device_id_type=MESH)
    for bb in (ahead, (b + blocks - 2) % blocks):
        for gg in (g, mate):
            pl.semaphore_signal(barrier, inc=1, device_id=(bb, gg), device_id_type=MESH)
    pl.semaphore_wait(barrier, 2 * groups + 3)

    def ints_copy(c):
        return remote(
            ints_ref.at[c], ints.at[0, rows(g)], h_send.at[c], h_recv.at[g],
            (plane + c % 2, c - c % 2 + x),
        )

    def to_self(c):
        return (core == x) & (c == own_c)

    order = [(2 * ((h + r) % pairs) + par) for r in range(pairs) for par in range(2)]
    for c in order:
        @pl.when(jnp.logical_not(to_self(c)))
        def _():
            ints_copy(c).start()

        @pl.when(to_self(c))
        def _():
            pltpu.make_async_copy(ints_ref.at[c], ints.at[0, rows(g)], h_recv.at[g]).start()

    own_metric = pltpu.make_async_copy(metric_ref, metric.at[rows(g)], own_sem)
    own_metric.start()

    def m1_copy(hv, r):
        return remote(
            metric_ref.at[pl.ds(pl.multiple_of(x * half, half), half), pl.ds(0, width(hv))],
            metric.at[halves(g, x), pl.ds(0, width(hv))],
            m1_send.at[r], m1_recv.at[hv],
            (b, 2 * ((h + r) % pairs) + core),
        )

    def m3_own(hv):
        return remote(
            metric_ref.at[:, pl.ds(0, width(hv))], metric.at[rows(g), pl.ds(0, width(hv))],
            m3_send.at[hv], m3_recv.at[hv], (b, mate),
        )

    def m2_copy(hv):
        piece = metric.at[halves(2 * hv + core, x), pl.ds(0, width(hv))]
        return remote(piece, piece, m2_send.at[hv], m2_recv.at[hv], (across, g))

    def m3_copy(hv):
        piece = metric.at[rows(2 * hv + core), pl.ds(0, width(hv))]
        return remote(piece, piece, m3_send.at[hv], m3_recv.at[hv], (b, mate))

    for hv in range(pairs):
        @pl.when(h == hv)
        def _():
            for r in range(1, pairs):
                m1_copy(hv, r).start()
            m3_own(hv).start()

    def z_copy(p):
        return remote(ints.at[0, rows(p)], ints.at[2, rows(p)], z_send.at[p], ring_recv.at[2, p], (ahead, g))

    def c_copy(p):
        return remote(ints.at[0, rows(p)], ints.at[1, rows(p)], c_send.at[p], ring_recv.at[1, p], (b, mate))

    def f_copy(p, role):
        return remote(ints.at[2, rows(p)], ints.at[role, rows(p)], f_send.at[p], ring_recv.at[role, p], (b, mate))

    def w_copy(p):
        return remote(ints.at[2, rows(p)], ints.at[3, rows(p)], w_send.at[p], ring_recv.at[3, p], (ahead, mate))

    for p in order:
        landed(ints.at[0, rows(p)], h_recv.at[p])
        z_copy(p).start()

        @pl.when(core == 0)
        def _():
            c_copy(p).start()

    for hv in range(pairs):
        @pl.when(h != hv)
        def _():
            landed(metric.at[halves(2 * hv + core, x), pl.ds(0, width(hv))], m1_recv.at[hv])
            m2_copy(hv).start()
    for hv in range(pairs):
        @pl.when(h != hv)
        def _():
            landed(metric.at[halves(2 * hv + core, 1 - x), pl.ds(0, width(hv))], m2_recv.at[hv])
            m3_copy(hv).start()

    for p in order:
        landed(ints.at[2, rows(p)], ring_recv.at[2, p])

        @pl.when(core == 1)
        def _():
            w_copy(p).start()
            f_copy(p, 1).start()

        @pl.when(core == 0)
        def _():
            f_copy(p, 3).start()

    own_metric.wait()
    for hv in range(pairs):
        landed(metric.at[rows(2 * hv + 1 - core), pl.ds(0, width(hv))], m3_recv.at[hv])

    levels = jnp.broadcast_to(vir_ref[...], (vir, vir))
    gap[...] = levels + levels.T

    def span(q):
        return pl.ds(pl.multiple_of(q * tile, tile), tile)

    @pl.loop(0, tiles)
    def _(p):
        @pl.loop(0, p + 1)
        def _(q):
            metric_t[span(q), span(p)] = metric[span(p), span(q)].T

    dens[...] = jnp.zeros_like(dens)
    own_energy = occ_ref[own_b * groups + own_c]

    @pl.loop(0, CYCLE)
    def _(k):
        role = (k % 2) * 2 + k // 2

        @pl.when(role % 2 == 1)
        def _():
            for p in range(groups):
                landed(ints.at[role, rows(p)], ring_recv.at[role, p])

        for q in range(tiles):
            low = q * tile
            fit[low:low + tile, :] = jnp.dot(
                metric_t[low:low + tile, low:], ints[role, low:, :],
                preferred_element_type=jnp.float32,
            ).astype(fit.dtype)

        @pl.when(k == 0)
        def _():
            @pl.loop(0, tiles)
            def _(q):
                fit_t[:, span(q)] = fit[span(q), :].T

        pair = jnp.dot(fit_t[...], fit[...], preferred_element_type=jnp.float32)
        energy = own_energy + occ_ref[(own_b + blocks - role) % blocks * groups + own_c]
        amplitude_t = ((2.0 * pair.T - pair) / (energy - gap[...])).astype(fit.dtype)

        @pl.loop(0, tiles)
        def _(q):
            dens[span(q), :] += jnp.dot(fit[span(q), :], amplitude_t, preferred_element_type=jnp.float32)

    dens_b[...] = dens[...].astype(dens_b.dtype)

    def g_copy(p):
        return remote(gam.at[rows(p)], out_ref.at[own_c], g_send.at[p], g_recv.at[own_c], (own_b, p))

    def g_self(p):
        return (core == x) & (g == p)

    for t in range(tiles):
        low = t * tile
        gam[low:low + tile, :] = jnp.dot(
            metric[low:low + tile, :low + tile], dens_b[:low + tile, :],
            preferred_element_type=jnp.float32,
        ).astype(gam.dtype)
        for p in range(low // shard, (low + tile) // shard):
            @pl.when(jnp.logical_not(g_self(p)))
            def _():
                g_copy(p).start()

            @pl.when(g_self(p))
            def _():
                pltpu.make_async_copy(gam.at[rows(p)], out_ref.at[own_c], g_recv.at[own_c]).start()

    for c in range(groups):
        @pl.when(jnp.logical_not(to_self(c)))
        def _():
            ints_copy(c).wait_send()
        z_copy(c).wait_send()

        @pl.when(core == 0)
        def _():
            c_copy(c).wait_send()
        f_copy(c, 1).wait_send()

        @pl.when(core == 1)
        def _():
            w_copy(c).wait_send()

        @pl.when(jnp.logical_not(g_self(c)))
        def _():
            g_copy(c).wait_send()
    for hv in range(pairs):
        @pl.when(h == hv)
        def _():
            for r in range(1, pairs):
                m1_copy(hv, r).wait_send()
            m3_own(hv).wait_send()

        @pl.when(h != hv)
        def _():
            m2_copy(hv).wait_send()
            m3_copy(hv).wait_send()
    for c in range(groups):
        landed(out_ref.at[c], g_recv.at[c])


def local(half_ints, metric_inv, occ_energy, vir_energy):
    groups, blocks = lax.axis_size("aux"), lax.axis_size("blk")
    shard, vir = half_ints.shape[1:]
    naux = metric_inv.shape[1]
    tile = shard if shard % 128 == 0 else naux // 4
    pairs = groups // 2
    dma = pltpu.SemaphoreType.DMA
    return pl.pallas_call(
        functools.partial(kernel, blocks, groups, tile),
        out_shape=jax.ShapeDtypeStruct(half_ints.shape, jnp.bfloat16),
        in_specs=[
            pl.BlockSpec(memory_space=pl.ANY),
            pl.BlockSpec(memory_space=pl.ANY),
            pl.BlockSpec(memory_space=pltpu.SMEM),
            pl.BlockSpec(memory_space=pltpu.VMEM),
        ],
        out_specs=pl.BlockSpec(memory_space=pl.ANY),
        scratch_shapes=[
            pltpu.VMEM((CYCLE, naux, vir), jnp.bfloat16),
            pltpu.VMEM((naux, naux), jnp.bfloat16),
            pltpu.VMEM((naux, naux), jnp.bfloat16),
            pltpu.VMEM((naux, vir), jnp.bfloat16),
            pltpu.VMEM((vir, naux), jnp.bfloat16),
            pltpu.VMEM((vir, vir), jnp.float32),
            pltpu.VMEM((naux, vir), jnp.float32),
            pltpu.VMEM((naux, vir), jnp.bfloat16),
            pltpu.VMEM((naux, vir), jnp.bfloat16),
            dma((groups,)), dma((groups,)), dma((groups,)), dma((groups,)), dma((groups,)),
            dma((groups,)), dma((CYCLE, groups)),
            dma((pairs,)), dma((pairs,)), dma((pairs,)), dma((pairs,)), dma((pairs,)), dma((pairs,)),
            dma(()), dma((groups,)), dma((groups,)),
        ],
        compiler_params=pltpu.CompilerParams(
            collective_id=0, has_side_effects=True, vmem_limit_bytes=56 * 2**20
        ),
    )(half_ints, metric_inv, occ_energy, vir_energy[None, :])


def solution(mesh):
    placed = (P("blk", "aux", None), P("aux", None), P(), P())
    return jax.shard_map(
        local, mesh=mesh, in_specs=placed, out_specs=P("blk", "aux", None), check_vma=False
    )
```

time: 200 us -> 87.6 us (0.44)
  waiting for transfers between devices: 89.3 us -> 0 us
  Pallas kernels: 0 us -> 83.8 us
  blocking collectives: 44.2 us -> 0 us
  matrix products: 26.7 us -> 0 us
  between operations: 18.5 us -> 0.01 us
  other arithmetic: 9.59 us -> 0 us
  local copies, waits for them, and re-layouts: 9.57 us -> 3.65 us
    pallas_call x0 -> x1, Pallas kernels: none -> 83.8 us  [local(): pl.pallas_call(functools.partial(kernel, blocks, groups, tile), out_shape...]
    ppermute x3 -> x0, waiting for transfers between devices: 67.7 us -> none  [shifted(): return lax.ppermute(block, axis, route)]
    all_to_all x2 -> x0, blocking collectives: 44.2 us -> none  [the longest x1 25.9 us: local(): lax.all_to_all(half_ints, 'aux', split_axis=0, concat_axis=1, tiled=True)]
    dot_general x9 -> x0, matrix products: 26.7 us -> none  [the longest x3 9.35 us: contribute(): jnp.einsum('uvab,vqb->uqa', amplitude, partner, preferred_element_type=jn...]
    all_gather x1 -> x0, waiting for transfers between devices: 20.9 us -> none  [local(): lax.all_gather(metric_inv, 'aux', axis=0, tiled=True)]
    unnamed x1 -> x0, other arithmetic: 9.05 us -> none
    convert_element_type x1 -> x0, local copies, waits for them, and re-layouts: 3.27 us -> none  [local(): gamma_local = jnp.einsum('pq,uqa->upa', lax.all_gather(metric_inv, 'aux',...]
  transfers between devices with their start and end apart: 4 -> 0, of which waited for: 4 -> 0; matrix products, arithmetic and copies ran while one was open for 8% -> 0% of each run, Pallas kernels for 0% -> 0%
where the time goes in v1:
time: 87.6 us; the launch traced here: 87.4 us
  Pallas kernels  83.8 us (96%)
  local copies, waits for them, and re-layouts  3.65 us (4%)
    pallas_call x1, Pallas kernels, local(): pl.pallas_call(functools.partial(kernel, blocks, groups, tile), out_shape...  83.8 us
    unnamed x1, local copies, waits for them, and re-layouts  2.4 us

profile of v1, /device:TPU:0, one launch (start us, length us, event | category | flops | bytes accessed | tf_op | source)
XLA Modules:
  0.0 87.4 jit_solution(17129069606559462812)
XLA Ops:
  0.0 1.2 %broadcast_in_dim.3.vir_ref = f32[1,384]{1,0:T(1,128)} reshape(f32[384]{0:T(512)} %param.7) | data formatting | bytes 3072 | tf_op jit(solution)/shard_map/broadcast_in_dim | solution.py:297
  1.2 83.8 %shard_map.46 = bf16[4,384,384]{2,1,0:T(8,128)(2,1)} custom-call(bf16[4,384,384]{2,1,0:T(8,128)(2,1)} %ints_ref.1, bf16[384,1536]{1,0:T(8,128)(2,1)} %metric_ref.1, f32[32]{0:T(128)} %occ_ref.1, f32[1,384]{1,0:T(1,128)} %broadcast_in_dim.3.vir_ref), custom_call_target="tpu_custom_call" | custom-call | tf_op jit(solution)/shard_map/pallas_call | solution.py:269
  85.0 2.4 %copy.6 = bf16[4,384,384]{2,1,0:T(8,128)(2,1)} copy(bf16[4,384,384]{2,1,0:T(8,128)(2,1)} %shard_map.46) | data formatting | bytes 2359296

commit v2 on v1

--- a/solution.py
+++ b/solution.py
@@ -21,6 +21,8 @@
 ):
     shard = ints_ref.shape[1]
     half = shard // 2
+    parts = 4 if half % 64 == 0 else 1
+    part = half // parts
     naux = metric_ref.shape[1]
     vir = ints_ref.shape[2]
     tiles = naux // tile
@@ -34,8 +36,8 @@
     def rows(p):
         return pl.ds(pl.multiple_of(p * shard, shard), shard)
 
-    def halves(p, which):
-        return pl.ds(pl.multiple_of(p * shard + which * half, half), half)
+    def slab(p, which, n):
+        return pl.ds(pl.multiple_of(p * shard + which * half + n * part, part), part)
 
     def width(hv):
         return min(naux, -(-2 * shard * (hv + 1) // tile) * tile)
@@ -70,23 +72,14 @@
         return (core == x) & (c == own_c)
 
     order = [(2 * ((h + r) % pairs) + par) for r in range(pairs) for par in range(2)]
-    for c in order:
-        @pl.when(jnp.logical_not(to_self(c)))
-        def _():
-            ints_copy(c).start()
-
-        @pl.when(to_self(c))
-        def _():
-            pltpu.make_async_copy(ints_ref.at[c], ints.at[0, rows(g)], h_recv.at[g]).start()
-
     own_metric = pltpu.make_async_copy(metric_ref, metric.at[rows(g)], own_sem)
     own_metric.start()
 
-    def m1_copy(hv, r):
+    def m1_copy(hv, r, n):
         return remote(
-            metric_ref.at[pl.ds(pl.multiple_of(x * half, half), half), pl.ds(0, width(hv))],
-            metric.at[halves(g, x), pl.ds(0, width(hv))],
-            m1_send.at[r], m1_recv.at[hv],
+            metric_ref.at[slab(0, x, n), pl.ds(0, width(hv))],
+            metric.at[slab(g, x, n), pl.ds(0, width(hv))],
+            m1_send.at[r, n], m1_recv.at[hv, n],
             (b, 2 * ((h + r) % pairs) + core),
         )
 
@@ -96,9 +89,9 @@
             m3_send.at[hv], m3_recv.at[hv], (b, mate),
         )
 
-    def m2_copy(hv):
-        piece = metric.at[halves(2 * hv + core, x), pl.ds(0, width(hv))]
-        return remote(piece, piece, m2_send.at[hv], m2_recv.at[hv], (across, g))
+    def m2_copy(hv, n):
+        piece = metric.at[slab(2 * hv + core, x, n), pl.ds(0, width(hv))]
+        return remote(piece, piece, m2_send.at[hv, n], m2_recv.at[hv, n], (across, g))
 
     def m3_copy(hv):
         piece = metric.at[rows(2 * hv + core), pl.ds(0, width(hv))]
@@ -108,8 +101,18 @@
         @pl.when(h == hv)
         def _():
             for r in range(1, pairs):
-                m1_copy(hv, r).start()
+                for n in range(parts):
+                    m1_copy(hv, r, n).start()
             m3_own(hv).start()
+
+    for c in order:
+        @pl.when(jnp.logical_not(to_self(c)))
+        def _():
+            ints_copy(c).start()
+
+        @pl.when(to_self(c))
+        def _():
+            pltpu.make_async_copy(ints_ref.at[c], ints.at[0, rows(g)], h_recv.at[g]).start()
 
     def z_copy(p):
         return remote(ints.at[0, rows(p)], ints.at[2, rows(p)], z_send.at[p], ring_recv.at[2, p], (ahead, g))
@@ -123,7 +126,7 @@
     def w_copy(p):
         return remote(ints.at[2, rows(p)], ints.at[3, rows(p)], w_send.at[p], ring_recv.at[3, p], (ahead, mate))
 
-    for p in order:
+    def pass_own(p):
         landed(ints.at[0, rows(p)], h_recv.at[p])
         z_copy(p).start()
 
@@ -131,18 +134,7 @@
         def _():
             c_copy(p).start()
 
-    for hv in range(pairs):
-        @pl.when(h != hv)
-        def _():
-            landed(metric.at[halves(2 * hv + core, x), pl.ds(0, width(hv))], m1_recv.at[hv])
-            m2_copy(hv).start()
-    for hv in range(pairs):
-        @pl.when(h != hv)
-        def _():
-            landed(metric.at[halves(2 * hv + core, 1 - x), pl.ds(0, width(hv))], m2_recv.at[hv])
-            m3_copy(hv).start()
-
-    for p in order:
+    def pass_on(p):
         landed(ints.at[2, rows(p)], ring_recv.at[2, p])
 
         @pl.when(core == 1)
@@ -153,6 +145,25 @@
         @pl.when(core == 0)
         def _():
             f_copy(p, 3).start()
+
+    for p in order[:2]:
+        pass_own(p)
+    for hv in range(pairs):
+        @pl.when(h != hv)
+        def _():
+            for n in range(parts):
+                landed(metric.at[slab(2 * hv + core, x, n), pl.ds(0, width(hv))], m1_recv.at[hv, n])
+                m2_copy(hv, n).start()
+    for p in order[:2]:
+        pass_on(p)
+    for hv in range(pairs):
+        @pl.when(h != hv)
+        def _():
+            for n in range(parts):
+                landed(metric.at[slab(2 * hv + core, 1 - x, n), pl.ds(0, width(hv))], m2_recv.at[hv, n])
+            m3_copy(hv).start()
+    for p in order[2:]:
+        pass_own(p)
 
     own_metric.wait()
     for hv in range(pairs):
@@ -170,12 +181,16 @@
         def _(q):
             metric_t[span(q), span(p)] = metric[span(p), span(q)].T
 
-    dens[...] = jnp.zeros_like(dens)
     own_energy = occ_ref[own_b * groups + own_c]
 
     @pl.loop(0, CYCLE)
     def _(k):
         role = (k % 2) * 2 + k // 2
+
+        @pl.when(k == 1)
+        def _():
+            for p in order[2:]:
+                pass_on(p)
 
         @pl.when(role % 2 == 1)
         def _():
@@ -199,11 +214,18 @@
         energy = own_energy + occ_ref[(own_b + blocks - role) % blocks * groups + own_c]
         amplitude_t = ((2.0 * pair.T - pair) / (energy - gap[...])).astype(fit.dtype)
 
-        @pl.loop(0, tiles)
-        def _(q):
-            dens[span(q), :] += jnp.dot(fit[span(q), :], amplitude_t, preferred_element_type=jnp.float32)
-
-    dens_b[...] = dens[...].astype(dens_b.dtype)
+        @pl.when(k == 0)
+        def _():
+            dens[...] = jnp.dot(fit[...], amplitude_t, preferred_element_type=jnp.float32)
+
+        @pl.when((k > 0) & (k < CYCLE - 1))
+        def _():
+            dens[...] += jnp.dot(fit[...], amplitude_t, preferred_element_type=jnp.float32)
+
+        @pl.when(k == CYCLE - 1)
+        def _():
+            total = dens[...] + jnp.dot(fit[...], amplitude_t, preferred_element_type=jnp.float32)
+            dens_b[...] = total.astype(dens_b.dtype)
 
     def g_copy(p):
         return remote(gam.at[rows(p)], out_ref.at[own_c], g_send.at[p], g_recv.at[own_c], (own_b, p))
@@ -248,12 +270,14 @@
         @pl.when(h == hv)
         def _():
             for r in range(1, pairs):
-                m1_copy(hv, r).wait_send()
+                for n in range(parts):
+                    m1_copy(hv, r, n).wait_send()
             m3_own(hv).wait_send()
 
         @pl.when(h != hv)
         def _():
-            m2_copy(hv).wait_send()
+            for n in range(parts):
+                m2_copy(hv, n).wait_send()
             m3_copy(hv).wait_send()
     for c in range(groups):
         landed(out_ref.at[c], g_recv.at[c])
@@ -265,6 +289,7 @@
     naux = metric_inv.shape[1]
     tile = shard if shard % 128 == 0 else naux // 4
     pairs = groups // 2
+    parts = 4 if shard % 128 == 0 else 1
     dma = pltpu.SemaphoreType.DMA
     return pl.pallas_call(
         functools.partial(kernel, blocks, groups, tile),
@@ -288,13 +313,13 @@
             pltpu.VMEM((naux, vir), jnp.bfloat16),
             dma((groups,)), dma((groups,)), dma((groups,)), dma((groups,)), dma((groups,)),
             dma((groups,)), dma((CYCLE, groups)),
-            dma((pairs,)), dma((pairs,)), dma((pairs,)), dma((pairs,)), dma((pairs,)), dma((pairs,)),
+            dma((pairs, parts)), dma((pairs, parts)), dma((pairs, parts)), dma((pairs, parts)), dma((pairs,)), dma((pairs,)),
             dma(()), dma((groups,)), dma((groups,)),
         ],
         compiler_params=pltpu.CompilerParams(
             collective_id=0, has_side_effects=True, vmem_limit_bytes=56 * 2**20
         ),
-    )(half_ints, metric_inv, occ_energy, vir_energy[None, :])
+    )(half_ints, metric_inv, occ_energy, vir_energy)
 
 
 def solution(mesh):

time: 87.6 us -> 78.8 us (0.90)
  Pallas kernels: 83.8 us -> 76.2 us
  local copies, waits for them, and re-layouts: 3.65 us -> 2.4 us
    pallas_call x1, Pallas kernels: 83.8 us -> 76.2 us  [local(): pl.pallas_call(functools.partial(kernel, blocks, groups, tile), out_shape...]
    broadcast_in_dim x1 -> x0, local copies, waits for them, and re-layouts: 1.24 us -> none  [local(): vir_energy[None, :]]
where the time goes in v2:
time: 78.8 us; the launch traced here: 78.6 us
  Pallas kernels  76.2 us (97%)
  local copies, waits for them, and re-layouts  2.4 us (3%)
    pallas_call x1, Pallas kernels, local(): pl.pallas_call(functools.partial(kernel, blocks, groups, tile), out_shape...  76.2 us
    unnamed x1, local copies, waits for them, and re-layouts  2.4 us

profile of v2, /device:TPU:0, one launch (start us, length us, event | category | flops | bytes accessed | tf_op | source)
XLA Modules:
  0.0 78.6 jit_solution(13482039766516115618)
XLA Ops:
  0.0 76.2 %shard_map.46 = bf16[4,384,384]{2,1,0:T(8,128)(2,1)} custom-call(bf16[4,384,384]{2,1,0:T(8,128)(2,1)} %ints_ref.1, bf16[384,1536]{1,0:T(8,128)(2,1)} %metric_ref.1, f32[32]{0:T(128)} %occ_ref.1, f32[384]{0:T(512)} %vir_ref.1), custom_call_target="tpu_custom_call" | custom-call | tf_op jit(solution)/shard_map/pallas_call | solution.py:294
  76.2 2.4 %copy.6 = bf16[4,384,384]{2,1,0:T(8,128)(2,1)} copy(bf16[4,384,384]{2,1,0:T(8,128)(2,1)} %shard_map.46) | data formatting | bytes 2359296
